TPU v7x, 32 devices: a whole 2x2x4 slice. The times are simulated.
32 devices in a mesh: groups: 2 (over y), row: 4 (over x, core), col: 4 (over z).
Axes of the slice: x: 2, y: 2, z: 4, core: 2. Of those that a mesh axis runs over, the one named last changes fastest.
Arguments:
- tiles: float32 [512, 128, 128], P(('groups', 'row', 'col')), parts along dimension 0, may hold values from 0 to 9
- tile_index: int32 [512, 2], P(('groups', 'row', 'col')), parts along dimension 0, may hold values from 0 to 3, as said below
- tile_count: int32 [32], P(('groups', 'row', 'col')), parts along dimension 0, may hold values from 4 to 16, as said below
- sources: int32 [16], P('groups'), parts along dimension 0, may hold values from 0 to 2047
Outputs:
- distance: float32 [16, 2048], P('groups', ('row', 'col')), parts along dimension 0
- path_counts: float32 [16, 2048], P('groups', ('row', 'col')), parts along dimension 0
- centrality: float32 [4096], P(('groups', 'row', 'col')), parts along dimension 0
There are 2 independent parts, one for each index of `groups`. A program takes and returns all parts, laid end to end along the dimension named above; each array names one. Nothing has to cross between parts.
Inputs may be any that keep to these rules, and one draw needn't show every extreme that they name: `tile_index`: entry (r, c) of a slot has r below 4 and c below 4; the 16 slots of one device name distinct pairs. `tile_count`: one entry per device; slots of a device from its count on hold only zeros; some device has all 16 slots live.
All inputs are finite; a program needn't handle non-finite values.
Results may differ from a plain program's by a relative error of at most 0.0003.
Values sent between devices are 32-bit elements; how exact they have to be, the bound alone decides.
A program may use at most 64 MiB of HBM per device.

v0:
```python
import functools

import jax
import jax.numpy as jnp
from jax import lax
from jax.experimental import pallas as pl
from jax.experimental.pallas import tpu as pltpu
from jax.sharding import PartitionSpec as P

LEVELS = 3
BACK = 2
CHUNK = 4

far_value = 1000000.0
no_edge = 2000000.0
half_far = 500000.0


def partner(me, step, count):
    if count & (count - 1):
        return (me + step) % count
    total = 0
    bit = 1
    while bit < count:
        total = total + ((me // bit) % 2 + (step // bit) % 2) % 2 * bit
        bit *= 2
    return total


def body(
    row_count,
    col_count,
    index_ref,
    count_ref,
    source_ref,
    tiles_ref,
    packed,
    raw,
    place_ref,
    weights,
    weights_back,
    partial,
    inbox,
    full,
    band,
    lower,
    sums_out,
    sums_all,
    sums_in,
    load_sem,
    all_send,
    all_recv,
    full_send,
    full_recv,
    col_send,
    col_recv,
):
    slot_total, tile_side = raw.shape[0], raw.shape[1]
    source_rows = source_ref.shape[0]
    my_row = lax.axis_index("row")
    my_col = lax.axis_index("col")
    positions = row_count * col_count
    row_chunk = CHUNK if row_count % CHUNK == 0 else 1
    col_chunk = CHUNK if col_count % CHUNK == 0 else 1
    wide = (source_rows, tile_side)
    pending = []

    def others():
        for col_step in reversed(range(col_count)):
            for row_step in reversed(range(row_count)):
                if row_step or col_step:
                    yield (
                        partner(my_row, row_step, row_count),
                        partner(my_col, col_step, col_count),
                        row_step,
                        col_step,
                    )

    load = pltpu.make_async_copy(tiles_ref, raw, load_sem)
    load.start()
    barrier = pltpu.get_barrier_semaphore()
    for other_row, other_col, _, _ in others():
        pl.semaphore_signal(
            barrier,
            inc=1,
            device_id={"row": other_row, "col": other_col},
            device_id_type=pl.DeviceIdType.MESH,
        )

    def start(source, target, send, recv, device):
        copy = pltpu.make_async_remote_copy(
            src_ref=source,
            dst_ref=target,
            send_sem=send,
            recv_sem=recv,
            device_id=device,
            device_id_type=pl.DeviceIdType.MESH,
        )
        copy.start()
        pending.append(copy)

    def push_all(stage, source_of, target):
        for other_row, other_col, row_step, col_step in others():
            start(
                source_of(other_row, other_col),
                target,
                all_send.at[stage, row_step, col_step],
                all_recv.at[stage, my_row, my_col],
                {"row": other_row, "col": other_col},
            )

    def arrived(target, recv, device):
        pltpu.make_async_remote_copy(
            src_ref=target,
            dst_ref=target,
            send_sem=load_sem,
            recv_sem=recv,
            device_id=device,
            device_id_type=pl.DeviceIdType.MESH,
        ).wait_recv()

    def source_mask(base):
        wanted = jnp.full(wide, -1, jnp.int32)
        for row in range(source_rows):
            wanted = jnp.where(sub == row, source_ref[row] - base, wanted)
        return lane == wanted

    def settle(found_dist, found_count, is_source):
        start_dist = jnp.where(is_source, 0.0, far_value).astype(jnp.float32)
        settled = jnp.minimum(start_dist, found_dist)
        ones = jnp.where(is_source, 1.0, 0.0).astype(jnp.float32)
        return settled, ones + jnp.where(found_dist == settled, found_count, 0.0)

    def combine(pieces):
        best, total = pieces[0]
        for other_best, other_total in pieces[1:]:
            both = jnp.minimum(best, other_best)
            total = jnp.where(best == both, total, 0.0) + jnp.where(
                other_best == both, other_total, 0.0
            )
            best = both
        return best, total

    live_count = count_ref[0]
    holds = []
    for slot in range(slot_total):
        position = index_ref[0, slot] * row_count + index_ref[1, slot]
        holds.append(jnp.where(slot < live_count, position, -1))

    def find_slot(position, carried):
        found = jnp.int32(-1)
        for slot in range(slot_total):
            found = jnp.where(holds[slot] == position, jnp.int32(slot), found)
        place_ref[position] = found
        return carried

    lax.fori_loop(0, positions, find_slot, 0)

    lane = lax.broadcasted_iota(jnp.int32, wide, 1)
    sub = lax.broadcasted_iota(jnp.int32, wide, 0)
    load.wait()

    band_base = my_row * col_count * tile_side

    def first_level(column, carried):
        best = jnp.full(wide, far_value, jnp.float32)
        for row in range(source_rows):
            place = source_ref[row] - band_base
            inside = (place >= 0) & (place < col_count * tile_side)
            place = jnp.clip(place, 0, col_count * tile_side - 1)
            slot = place_ref[(place // tile_side) * row_count + column]
            line = raw[jnp.maximum(slot, 0), pl.ds(place % tile_side, 1), :]
            limit = jnp.where(inside & (slot >= 0), 0.0, far_value).astype(jnp.float32)
            best = jnp.where((sub == row) & (line > limit), line, best)
        partial[0, column, 0] = best
        return carried

    lax.fori_loop(0, row_count, first_level, 0)
    inbox[0, my_col, my_row, 0] = partial[0, my_row, 0]
    pl.semaphore_wait(barrier, row_count * col_count - 1)
    push_all(
        0, lambda other_row, other_col: partial.at[0, other_row, 0], inbox.at[0, my_col, my_row, 0]
    )

    def prepare(position, carried):
        slot = place_ref[position]
        tile = raw[jnp.maximum(slot, 0)]
        limit = jnp.where(slot >= 0, 0.0, far_value).astype(jnp.float32)
        weights[position] = jnp.where(tile > limit, tile, no_edge)
        return carried

    lax.fori_loop(0, positions, prepare, 0)

    def turn(position, carried):
        weights_back[position] = weights[position].T
        return carried

    def band_block(stage, block, step):
        for row_step in range(row_count):
            giver = partner(my_row, row_step, row_count)

            def wait():
                piece = inbox.at[stage, block, giver]
                arrived(
                    piece.at[0] if stage in (0, LEVELS - 1) else piece,
                    all_recv.at[stage, giver, block],
                    {"row": giver, "col": block},
                )

            if row_step == 0:
                pl.when(step > 0)(wait)
            else:
                wait()
        is_source = source_mask((my_row * col_count + block) * tile_side)
        if stage in (0, LEVELS - 1):
            best = inbox[stage, block, 0, 0]
            for giver in range(1, row_count):
                best = jnp.minimum(best, inbox[stage, block, giver, 0])
            best = jnp.where(is_source, 0.0, best)
            return best, jnp.where(best < half_far, 1.0, 0.0).astype(jnp.float32)
        found = combine([(inbox[stage, block, g, 0], inbox[stage, block, g, 1]) for g in range(row_count)])
        return settle(*found, is_source)

    def forward(level):
        best_ref = partial.at[level]

        def clear(column, carried):
            best_ref[column, 0] = jnp.full(wide, far_value, jnp.float32)
            best_ref[column, 1] = jnp.zeros(wide, jnp.float32)
            return carried

        lax.fori_loop(0, row_count, clear, 0)

        def from_block(step, carried):
            block = partner(my_col, step, col_count)

            near_dist, near_count = band_block(level - 1, block, step)

            def columns(group, carried):
                first = group * row_chunk
                place = block * row_count + first
                before = [best_ref[first + t, 0] for t in range(row_chunk)]
                best = list(before)
                for u in range(tile_side):
                    wide_dist = jnp.broadcast_to(near_dist[:, u : u + 1], wide)
                    for t in range(row_chunk):
                        line = weights[place + t, u : u + 1, :]
                        best[t] = jnp.minimum(best[t], wide_dist + line)
                total = [
                    jnp.where(before[t] == best[t], best_ref[first + t, 1], 0.0)
                    for t in range(row_chunk)
                ]
                for u in range(tile_side):
                    wide_dist = jnp.broadcast_to(near_dist[:, u : u + 1], wide)
                    wide_count = jnp.broadcast_to(near_count[:, u : u + 1], wide)
                    for t in range(row_chunk):
                        line = weights[place + t, u : u + 1, :]
                        total[t] += jnp.where(wide_dist + line == best[t], wide_count, 0.0)
                for t in range(row_chunk):
                    best_ref[first + t, 0] = best[t]
                    best_ref[first + t, 1] = total[t]
                return carried

            return lax.fori_loop(0, row_count // row_chunk, columns, carried)

        lax.fori_loop(0, col_count, from_block, 0)
        inbox[level, my_col, my_row] = best_ref[my_row]
        if level == LEVELS - 1:
            push_all(
                level,
                lambda other_row, other_col: best_ref.at[other_row, 0],
                inbox.at[level, my_col, my_row, 0],
            )
        else:
            push_all(
                level,
                lambda other_row, other_col: best_ref.at[other_row],
                inbox.at[level, my_col, my_row],
            )

    lax.fori_loop(0, positions, turn, 0)
    for level in range(1, LEVELS):
        forward(level)

    last = LEVELS - 1
    full[my_row] = partial[last]
    for row_step in reversed(range(1, row_count)):
        other = partner(my_row, row_step, row_count)
        start(
            partial.at[last],
            full.at[my_row],
            full_send.at[row_step],
            full_recv.at[my_row],
            {"row": other, "col": my_col},
        )
    for row_step in range(1, row_count):
        other = partner(my_row, row_step, row_count)
        arrived(full.at[other], full_recv.at[other], {"row": other, "col": my_col})

    def settle_column(column, carried):
        found = combine([(full[g, column, 0], full[g, column, 1]) for g in range(row_count)])
        base = (column * col_count + my_col) * tile_side
        lower[0, column], lower[1, column] = settle(*found, source_mask(base))
        return carried

    lax.fori_loop(0, row_count, settle_column, 0)
    own_dist = lower[0, my_row]
    own_paths = lower[1, my_row]
    packed[0] = jnp.where(own_dist < half_far, own_dist, -1.0)
    packed[1] = own_paths

    def settle_block(step, carried):
        block = partner(my_col, step, col_count)
        band[block] = band_block(last, block, step)[0]
        return carried

    lax.fori_loop(0, col_count, settle_block, 0)

    for back in range(BACK):

        def clear(block, carried):
            sums_out[back, block] = jnp.zeros(wide, jnp.float32)
            return carried

        lax.fori_loop(0, col_count, clear, 0)

        def from_column(step, carried):
            column = partner(my_row, step, row_count)
            low_dist = lower[0, column]
            low_paths = lower[1, column]
            if back == 0:
                dependency = 0.0
            else:
                summed = jnp.zeros(wide, jnp.float32)
                for col_step in range(col_count):
                    giver = partner(my_col, col_step, col_count)

                    def wait():
                        arrived(
                            sums_all.at[column, giver],
                            all_recv.at[LEVELS, column, giver],
                            {"row": column, "col": giver},
                        )

                    if col_step == 0:
                        pl.when(step > 0)(wait)
                    else:
                        wait()
                for giver in range(col_count):
                    summed += sums_all[column, giver]
                dependency = low_paths * summed
            low_coef = jnp.where(
                low_paths > 0.5, (1.0 + dependency) / jnp.maximum(low_paths, 1.0), 0.0
            )

            def blocks(group, carried):
                first = group * col_chunk
                upper = [band[first + t] for t in range(col_chunk)]
                total = [sums_out[back, first + t] for t in range(col_chunk)]
                for v in range(tile_side):
                    wide_dist = jnp.broadcast_to(low_dist[:, v : v + 1], wide)
                    wide_coef = jnp.broadcast_to(low_coef[:, v : v + 1], wide)
                    for t in range(col_chunk):
                        line = weights_back[(first + t) * row_count + column, v : v + 1, :]
                        total[t] += jnp.where(upper[t] + line == wide_dist, wide_coef, 0.0)
                for t in range(col_chunk):
                    sums_out[back, first + t] = total[t]
                return carried

            return lax.fori_loop(0, col_count // col_chunk, blocks, carried)

        lax.fori_loop(0, row_count, from_column, 0)
        if back == 0:
            sums_all[my_row, my_col] = sums_out[0, my_col]
            push_all(
                LEVELS,
                lambda other_row, other_col: sums_out.at[0, other_col],
                sums_all.at[my_row, my_col],
            )
    for col_step in reversed(range(1, col_count)):
        other = partner(my_col, col_step, col_count)
        start(
            sums_out.at[1, other],
            sums_in.at[my_col],
            col_send.at[col_step],
            col_recv.at[my_col],
            {"row": my_row, "col": other},
        )
    summed = sums_out[1, my_col]
    for col_step in range(1, col_count):
        other = partner(my_col, col_step, col_count)
        arrived(sums_in.at[other], col_recv.at[other], {"row": my_row, "col": other})
        summed += sums_in[other]
    own_source = source_mask((my_row * col_count + my_col) * tile_side)
    packed[2] = jnp.where(own_source, 0.0, own_paths * summed)
    for copy in pending:
        copy.wait_send()


def unpack(packed, dist_out, path_out, cent_out):
    dist_out[...] = packed[0]
    path_out[...] = packed[1]
    cent_out[...] = jnp.sum(packed[2], axis=0, keepdims=True) / packed.shape[1]


def solution(mesh):
    row_count = mesh.shape["row"]
    col_count = mesh.shape["col"]

    def per_device(tiles, tile_index, tile_count, sources):
        slot_total, tile_side = tiles.shape[0], tiles.shape[1]
        source_rows = sources.shape[0]
        wide = (source_rows, tile_side)
        positions = row_count * col_count
        vector = pl.BlockSpec(memory_space=pltpu.VMEM)
        scalar = pl.BlockSpec(memory_space=pltpu.SMEM)
        packed = pl.pallas_call(
            functools.partial(body, row_count, col_count),
            out_shape=jax.ShapeDtypeStruct((3,) + wide, jnp.float32),
            in_specs=[scalar, scalar, scalar, pl.BlockSpec(memory_space=pl.ANY)],
            out_specs=vector,
            scratch_shapes=[
                pltpu.VMEM((slot_total, tile_side, tile_side), jnp.float32),
                pltpu.SMEM((positions,), jnp.int32),
                pltpu.VMEM((positions, tile_side, tile_side), jnp.float32),
                pltpu.VMEM((positions, tile_side, tile_side), jnp.float32),
                pltpu.VMEM((LEVELS, row_count, 2) + wide, jnp.float32),
                pltpu.VMEM((LEVELS, col_count, row_count, 2) + wide, jnp.float32),
                pltpu.VMEM((row_count, row_count, 2) + wide, jnp.float32),
                pltpu.VMEM((col_count,) + wide, jnp.float32),
                pltpu.VMEM((2, row_count) + wide, jnp.float32),
                pltpu.VMEM((BACK, col_count) + wide, jnp.float32),
                pltpu.VMEM((row_count, col_count) + wide, jnp.float32),
                pltpu.VMEM((col_count,) + wide, jnp.float32),
                pltpu.SemaphoreType.DMA,
                pltpu.SemaphoreType.DMA((LEVELS + 1, row_count, col_count)),
                pltpu.SemaphoreType.DMA((LEVELS + 1, row_count, col_count)),
                pltpu.SemaphoreType.DMA((row_count,)),
                pltpu.SemaphoreType.DMA((row_count,)),
                pltpu.SemaphoreType.DMA((col_count,)),
                pltpu.SemaphoreType.DMA((col_count,)),
            ],
            compiler_params=pltpu.CompilerParams(
                collective_id=0,
                has_side_effects=True,
            ),
        )(tile_index.T, tile_count, sources, tiles)
        distance, paths, centrality = pl.pallas_call(
            unpack,
            out_shape=(
                jax.ShapeDtypeStruct(wide, jnp.float32),
                jax.ShapeDtypeStruct(wide, jnp.float32),
                jax.ShapeDtypeStruct((1, tile_side), jnp.float32),
            ),
            in_specs=[vector],
            out_specs=(vector, vector, vector),
        )(packed)
        return distance, paths, centrality.reshape(tile_side)

    in_specs = (
        P(("groups", "row", "col"), None, None),
        P(("groups", "row", "col"), None),
        P(("groups", "row", "col")),
        P("groups"),
    )
    out_specs = (
        P("groups", ("row", "col")),
        P("groups", ("row", "col")),
        P(("groups", "row", "col")),
    )
    return jax.shard_map(
        per_device, mesh=mesh, in_specs=in_specs, out_specs=out_specs, check_vma=False
    )
```

profile of v0, /device:TPU:0, one launch (start us, length us, event | category | flops | bytes accessed | tf_op | source)
XLA Modules:
  0.0 38.2 jit_solution(8678876949429006133)
XLA Ops:
  1.3 35.6 %shard_map.67.packed = f32[3,8,128]{2,1,0:T(8,128)} custom-call(s32[2,16]{1,0:T(2,128)} %bitcast.2, s32[1]{0:T(128)S(6)} %copy.7.count_ref, s32[8]{0:T(128)} %source_ref.1, f32[16,128,128]{2,1,0:T(8,128)} %tiles_ref.1), custom_call_target="tpu_custom_call" | custom-call | tf_op jit(solution)/shard_map/pallas_call | solution.py:417
  36.9 1.3 %shard_map.68 = (f32[8,128]{1,0:T(8,128)}, f32[8,128]{1,0:T(8,128)}, f32[1,128]{1,0:T(1,128)}) custom-call(f32[3,8,128]{2,1,0:T(8,128)} %shard_map.67.packed), custom_call_target="tpu_custom_call" | custom-call | tf_op jit(solution)/shard_map/pallas_call | solution.py:448
where the time goes:
time: 38.5 us; the launch traced here: 38.2 us
  Pallas kernels  36.9 us (96%)
  between operations  1.29 us (3%)
    pallas_call x1, Pallas kernels, per_device(): pl.pallas_call(functools.partial(body, row_count, col_count), out_shape=j...  35.6 us
    pallas_call x1, Pallas kernels, per_device(): pl.pallas_call(unpack, out_shape=(jax.ShapeDtypeStruct(wide, jnp.float32)...  1.31 us

commit v1 on v0

v1 whole, which is shorter than its diff:
```python
import functools

import jax
import jax.numpy as jnp
from jax import lax
from jax.experimental import pallas as pl
from jax.experimental.pallas import tpu as pltpu
from jax.sharding import PartitionSpec as P

LEVELS = 3
BACK = 2
CHUNK = 4
PAIR = 2
SUB = 8
MASK_TILES = 32

far_value = 1000000.0
no_edge = 2000000.0
half_far = 500000.0
scale_up = 2.0**60


def partner(me, step, count):
    if count & (count - 1):
        return (me + step) % count
    total = 0
    bit = 1
    while bit < count:
        total = total + ((me // bit) % 2 + (step // bit) % 2) % 2 * bit
        bit *= 2
    return total


def fold(parts, join, sub):
    half = SUB // 2
    while len(parts) > 1:
        low = sub % (2 * half) < half
        count = len(parts) // 2
        parts = [
            join(
                jnp.where(low, parts[k], parts[k + count]),
                pltpu.roll(jnp.where(low, parts[k + count], parts[k]), half, 0)
                if half * 2 == SUB
                else jnp.where(
                    low,
                    pltpu.roll(parts[k], SUB - half, 0),
                    pltpu.roll(parts[k + count], half, 0),
                ),
            )
            for k in range(count)
        ]
        half //= 2
    return parts[0]


def body(
    row_count,
    col_count,
    index_hbm,
    count_hbm,
    source_hbm,
    tiles_ref,
    packed,
    index_ref,
    count_ref,
    source_ref,
    raw,
    place_ref,
    weights,
    weights_back,
    pick,
    lanes,
    lanes_more,
    masks,
    gathered,
    dist_out,
    count_out,
    dist_in,
    count_in,
    full_dist,
    full_count,
    band,
    lower,
    sums_out,
    sums_all,
    sums_in,
    load_sem,
    small_sem,
    all_send,
    all_recv,
    full_send,
    full_recv,
    col_send,
    col_recv,
):
    slot_total, tile_side = raw.shape[0], raw.shape[1]
    source_rows = source_ref.shape[0]
    my_row = lax.axis_index("row")
    my_col = lax.axis_index("col")
    positions = row_count * col_count
    row_chunk = CHUNK if row_count % CHUNK == 0 else 1
    row_pair = PAIR if row_count % PAIR == 0 else 1
    col_pair = PAIR if col_count % PAIR == 0 else 1
    groups = tile_side // SUB
    wide = (source_rows, tile_side)
    last = LEVELS - 1
    keep_masks = masks.shape[0] == positions
    pending = []

    def others():
        for col_step in reversed(range(col_count)):
            for row_step in reversed(range(row_count)):
                if row_step or col_step:
                    yield (
                        partner(my_row, row_step, row_count),
                        partner(my_col, col_step, col_count),
                        row_step,
                        col_step,
                    )

    small = [
        pltpu.make_async_copy(index_hbm, index_ref, small_sem.at[0]),
        pltpu.make_async_copy(count_hbm, count_ref, small_sem.at[1]),
        pltpu.make_async_copy(source_hbm, source_ref, small_sem.at[2]),
    ]
    for copy in small:
        copy.start()
    load = pltpu.make_async_copy(tiles_ref, raw, load_sem)
    load.start()
    barrier = pltpu.get_barrier_semaphore()
    for other_row, other_col, _, _ in others():
        pl.semaphore_signal(
            barrier,
            inc=1,
            device_id={"row": other_row, "col": other_col},
            device_id_type=pl.DeviceIdType.MESH,
        )

    def start(source, target, send, recv, device):
        copy = pltpu.make_async_remote_copy(
            src_ref=source,
            dst_ref=target,
            send_sem=send,
            recv_sem=recv,
            device_id=device,
            device_id_type=pl.DeviceIdType.MESH,
        )
        copy.start()
        pending.append(copy)

    def push_all(stage, source_of, target, with_own_col=True):
        for other_row, other_col, row_step, col_step in others():
            if col_step or with_own_col:
                start(
                    source_of(other_row, other_col),
                    target,
                    all_send.at[stage, row_step, col_step],
                    all_recv.at[stage, my_row, my_col],
                    {"row": other_row, "col": other_col},
                )

    def push_full(stage, source, target):
        target[my_row] = source[...]
        for row_step in reversed(range(1, row_count)):
            start(
                source,
                target.at[my_row],
                full_send.at[stage, row_step],
                full_recv.at[stage, my_row],
                {"row": partner(my_row, row_step, row_count), "col": my_col},
            )

    def arrived(target, recv, device):
        pltpu.make_async_remote_copy(
            src_ref=target,
            dst_ref=target,
            send_sem=load_sem,
            recv_sem=recv,
            device_id=device,
            device_id_type=pl.DeviceIdType.MESH,
        ).wait_recv()

    def full_arrived(stage, target):
        for row_step in range(1, row_count):
            other = partner(my_row, row_step, row_count)
            arrived(target.at[other], full_recv.at[stage, other], {"row": other, "col": my_col})

    def block_arrived(stage, target, block, own):
        for row_step in range(row_count):
            giver = partner(my_row, row_step, row_count)

            def wait():
                arrived(
                    target.at[block, giver],
                    all_recv.at[stage, giver, block],
                    {"row": giver, "col": block},
                )

            if row_step == 0 and own is not None:
                pl.when(jnp.logical_not(own))(wait)
            else:
                wait()

    def source_mask(base):
        wanted = jnp.full(wide, -1, jnp.int32)
        for row in range(source_rows):
            wanted = jnp.where(sub == row, source_ref[row] - base, wanted)
        return lane == wanted

    def settle(found_dist, found_count, is_source):
        start_dist = jnp.where(is_source, 0.0, far_value).astype(jnp.float32)
        settled = jnp.minimum(start_dist, found_dist)
        ones = jnp.where(is_source, 1.0, 0.0).astype(jnp.float32)
        return settled, ones + jnp.where(found_dist == settled, found_count, 0.0)

    def nearest(values):
        return functools.reduce(jnp.minimum, values)

    def combine(dists, counts):
        best = nearest(dists)
        total = functools.reduce(
            jnp.add, [jnp.where(d == best, n, 0.0) for d, n in zip(dists, counts, strict=True)]
        )
        return best, total

    def spread(value, target):
        scaled = value * scale_up
        high = scaled.astype(jnp.bfloat16).astype(jnp.float32)
        rest = scaled - high
        middle = rest.astype(jnp.bfloat16).astype(jnp.float32)
        pieces = jnp.concatenate([high, middle, rest - middle, jnp.zeros_like(high)], axis=0)
        target[...] = lax.dot_general(
            pieces.astype(jnp.bfloat16),
            pick[...],
            (((0,), (0,)), ((), ())),
            preferred_element_type=jnp.float32,
        )

    def spread_at(ref, place, group, s):
        return ref[
            place, group * SUB : (group + 1) * SUB, s * tile_side : (s + 1) * tile_side
        ]

    for copy in small:
        copy.wait()
    live_count = count_ref[0]
    holds = []
    for slot in range(slot_total):
        position = index_ref[0, slot] * row_count + index_ref[1, slot]
        holds.append(jnp.where(slot < live_count, position, -1))

    def find_slot(position, carried):
        found = jnp.int32(-1)
        for slot in range(slot_total):
            found = jnp.where(holds[slot] == position, jnp.int32(slot), found)
        place_ref[position] = found
        return carried

    lax.fori_loop(0, positions, find_slot, 0)

    lane = lax.broadcasted_iota(jnp.int32, wide, 1)
    sub = lax.broadcasted_iota(jnp.int32, wide, 0)
    load.wait()

    band_base = my_row * col_count * tile_side

    part_row = lax.broadcasted_iota(jnp.int32, pick.shape, 0)
    part_source = lax.broadcasted_iota(jnp.int32, pick.shape, 1) // tile_side
    chosen = (part_row % source_rows == part_source) & (part_row < 3 * source_rows)
    pick[...] = jnp.where(chosen, 1.0 / scale_up, 0.0).astype(jnp.bfloat16)

    def first_level(column, carried):
        best = jnp.full(wide, far_value, jnp.float32)
        for row in range(source_rows):
            place = source_ref[row] - band_base
            inside = (place >= 0) & (place < col_count * tile_side)
            place = jnp.clip(place, 0, col_count * tile_side - 1)
            slot = place_ref[(place // tile_side) * row_count + column]
            line = raw[jnp.maximum(slot, 0), pl.ds(place % tile_side, 1), :]
            limit = jnp.where(inside & (slot >= 0), 0.0, far_value).astype(jnp.float32)
            best = jnp.where((sub == row) & (line > limit), line, best)
        dist_out[0, column] = best
        return carried

    lax.fori_loop(0, row_count, first_level, 0)
    dist_in[0, my_col, my_row] = dist_out[0, my_row]
    pl.semaphore_wait(barrier, row_count * col_count - 1)
    push_all(0, lambda other_row, other_col: dist_out.at[0, other_row], dist_in.at[0, my_col, my_row])

    def prepare(position, carried):
        slot = place_ref[position]
        tile = raw[jnp.maximum(slot, 0)]
        limit = jnp.where(slot >= 0, 0.0, far_value).astype(jnp.float32)
        weights[position] = jnp.where(tile > limit, tile, no_edge)
        return carried

    lax.fori_loop(0, positions, prepare, 0)

    def turn(position, carried):
        weights_back[position] = weights[position].T
        return carried

    lax.fori_loop(0, positions, turn, 0)

    def relax(block):
        def columns(chunk, carried):
            first = chunk * row_chunk
            best = [[gathered[first + t, s] for s in range(source_rows)] for t in range(row_chunk)]
            for group in range(groups):
                lines = [
                    weights[block * row_count + first + t, group * SUB : (group + 1) * SUB, :]
                    for t in range(row_chunk)
                ]
                for s in range(source_rows):
                    near = spread_at(lanes, block, group, s)
                    for t in range(row_chunk):
                        best[t][s] = jnp.minimum(best[t][s], near + lines[t])
            for t in range(row_chunk):
                for s in range(source_rows):
                    gathered[first + t, s] = best[t][s]
            return carried

        lax.fori_loop(0, row_count // row_chunk, columns, 0)

    def tally(level, block):
        def columns(chunk, carried):
            first = chunk * row_pair
            total = [[gathered[first + t, s] for s in range(source_rows)] for t in range(row_pair)]
            best = [
                [
                    jnp.broadcast_to(dist_out[level, first + t, s : s + 1, :], (SUB, tile_side))
                    for s in range(source_rows)
                ]
                for t in range(row_pair)
            ]
            for group in range(groups):
                lines = [
                    weights[block * row_count + first + t, group * SUB : (group + 1) * SUB, :]
                    for t in range(row_pair)
                ]
                for s in range(source_rows):
                    near = spread_at(lanes, block, group, s)
                    paths = 1.0 if level == 1 else spread_at(lanes_more, block, group, s)
                    for t in range(row_pair):
                        total[t][s] += jnp.where(near + lines[t] == best[t][s], paths, 0.0)
            for t in range(row_pair):
                for s in range(source_rows):
                    gathered[first + t, s] = total[t][s]
            return carried

        lax.fori_loop(0, row_count // row_pair, columns, 0)

    def fill(count, value):
        def one(place, carried):
            for s in range(source_rows):
                gathered[place, s] = jnp.full((SUB, tile_side), value, jnp.float32)
            return carried

        lax.fori_loop(0, count, one, 0)

    def forward(level):
        fill(row_count, far_value)

        def relax_block(step, carried):
            block = partner(my_col, step, col_count)
            block_arrived(level - 1, dist_in.at[level - 1], block, step == 0)
            best = nearest([dist_in[level - 1, block, g] for g in range(row_count)])
            is_source = source_mask((my_row * col_count + block) * tile_side)
            spread(jnp.where(is_source, 0.0, best), lanes.at[block])
            relax(block)
            return carried

        lax.fori_loop(0, col_count, relax_block, 0)

        def close_dist(column, carried):
            dist_out[level, column] = fold(
                [gathered[column, s] for s in range(source_rows)], jnp.minimum, sub
            )
            return carried

        lax.fori_loop(0, row_count, close_dist, 0)
        if level == last:
            push_full(0, dist_out.at[level], full_dist)
        else:
            dist_in[level, my_col, my_row] = dist_out[level, my_row]
        push_all(
            level,
            lambda other_row, other_col: dist_out.at[level, other_row],
            dist_in.at[level, my_col, my_row],
            level != last,
        )

        fill(row_count, 0.0)

        def tally_blocks(pair, carried):
            blocks = [partner(my_col, pair * col_pair + t, col_count) for t in range(col_pair)]
            if level > 1:
                for t, block in enumerate(blocks):
                    block_arrived(LEVELS, count_in, block, (pair == 0) if t == 0 else None)
                for block in blocks:
                    found = combine(
                        [dist_in[level - 1, block, g] for g in range(row_count)],
                        [count_in[block, g] for g in range(row_count)],
                    )
                    is_source = source_mask((my_row * col_count + block) * tile_side)
                    spread(settle(*found, is_source)[1], lanes_more.at[block])
            for block in blocks:
                tally(level, block)
            return carried

        lax.fori_loop(0, col_count // col_pair, tally_blocks, 0)

        def close_count(column, carried):
            total = fold([gathered[column, s] for s in range(source_rows)], jnp.add, sub)
            if level == 1:
                total = jnp.where(dist_out[level, column] < half_far, total, 0.0)
            count_out[level - 1, column] = total
            return carried

        lax.fori_loop(0, row_count, close_count, 0)
        if level == last:
            push_full(1, count_out.at[level - 1], full_count)
        else:
            count_in[my_col, my_row] = count_out[level - 1, my_row]
            push_all(
                LEVELS,
                lambda other_row, other_col: count_out.at[level - 1, other_row],
                count_in.at[my_col, my_row],
            )

    for level in range(1, LEVELS):
        forward(level)

    full_arrived(0, full_dist)

    def lower_dist(chunk, carried):
        for t in range(row_chunk):
            column = chunk * row_chunk + t
            best = nearest([full_dist[g, column] for g in range(row_count)])
            is_source = source_mask((column * col_count + my_col) * tile_side)
            settled = jnp.where(is_source, 0.0, best)
            lower[0, column] = settled
            spread(settled, lanes.at[column])
        return carried

    lax.fori_loop(0, row_count // row_chunk, lower_dist, 0)

    def settle_upper(block):
        for row_step in range(row_count):
            giver = partner(my_row, row_step, row_count)
            arrived(
                dist_in.at[last, block, giver],
                all_recv.at[last, giver, block],
                {"row": giver, "col": block},
            )
        best = nearest([dist_in[last, block, g] for g in range(row_count)])
        is_source = source_mask((my_row * col_count + block) * tile_side)
        band[block] = jnp.where(is_source, 0.0, best)

    def upper_lines(block):
        return [
            jnp.broadcast_to(band[block, s : s + 1, :], (SUB, tile_side)) for s in range(source_rows)
        ]

    def compare(block, column, group, upper, visit):
        line = weights_back[block * row_count + column, group * SUB : (group + 1) * SUB, :]
        for s in range(source_rows):
            visit(s, upper[s] + line == spread_at(lanes, column, group, s))

    for col_step in range(col_count):
        block = partner(my_col, col_step, col_count)
        if col_step:
            settle_upper(block)
        else:
            band[block] = lower[0, my_row]
        if keep_masks:

            def mark(column, carried, block=block):
                upper = upper_lines(block)
                for group in range(groups):

                    def keep(s, same, group=group):
                        masks[block * row_count + column, group, s] = jnp.where(same, 1.0, 0.0)

                    compare(block, column, group, upper, keep)
                return carried

            lax.fori_loop(0, row_count, mark, 0)

    def add_shares(block, column, total, upper):
        for group in range(groups):
            if keep_masks:
                for s in range(source_rows):
                    share = spread_at(lanes_more, column, group, s)
                    total[s] += masks[block * row_count + column, group, s] * share
            else:

                def add(s, same, group=group):
                    share = spread_at(lanes_more, column, group, s)
                    total[s] += jnp.where(same, share, 0.0)

                compare(block, column, group, upper, add)

    def coefficient(column, dependency):
        paths = lower[1, column]
        spread(
            jnp.where(paths > 0.5, (1.0 + dependency) / jnp.maximum(paths, 1.0), 0.0),
            lanes_more.at[column],
        )

    full_arrived(1, full_count)

    def lower_paths(chunk, carried):
        for t in range(row_chunk):
            column = chunk * row_chunk + t
            found = combine(
                [full_dist[g, column] for g in range(row_count)],
                [full_count[g, column] for g in range(row_count)],
            )
            is_source = source_mask((column * col_count + my_col) * tile_side)
            lower[1, column] = settle(*found, is_source)[1]
            coefficient(column, 0.0)
        return carried

    lax.fori_loop(0, row_count // row_chunk, lower_paths, 0)

    for col_step in reversed(range(col_count)):
        block = partner(my_col, col_step, col_count)

        def first_sums(column, total, block=block):
            total = list(total)
            add_shares(block, column, total, None if keep_masks else upper_lines(block))
            return tuple(total)

        total = lax.fori_loop(
            0,
            row_count,
            first_sums,
            tuple(jnp.zeros((SUB, tile_side), jnp.float32) for _ in range(source_rows)),
        )
        sums_out[0, block] = fold(list(total), jnp.add, sub)
        for row_step in reversed(range(row_count)):
            if row_step or col_step:
                other = partner(my_row, row_step, row_count)
                start(
                    sums_out.at[0, block],
                    sums_all.at[my_row, my_col],
                    all_send.at[LEVELS + 1, row_step, col_step],
                    all_recv.at[LEVELS + 1, my_row, my_col],
                    {"row": other, "col": block},
                )
            else:
                sums_all[my_row, my_col] = sums_out[0, block]

    packed[0] = jnp.where(lower[0, my_row] < half_far, lower[0, my_row], -1.0)
    packed[1] = lower[1, my_row]
    fill(col_count, 0.0)

    def from_columns(pair, carried):
        columns = [partner(my_row, pair * row_pair + t, row_count) for t in range(row_pair)]
        for t, column in enumerate(columns):
            for col_step in range(col_count):
                giver = partner(my_col, col_step, col_count)

                def wait(column=column, giver=giver):
                    arrived(
                        sums_all.at[column, giver],
                        all_recv.at[LEVELS + 1, column, giver],
                        {"row": column, "col": giver},
                    )

                if col_step == 0 and t == 0:
                    pl.when(pair > 0)(wait)
                else:
                    wait()
        for column in columns:
            summed = functools.reduce(jnp.add, [sums_all[column, g] for g in range(col_count)])
            coefficient(column, lower[1, column] * summed)

        def one_block(block, carried):
            total = [gathered[block, s] for s in range(source_rows)]
            upper = None if keep_masks else upper_lines(block)
            for column in columns:
                add_shares(block, column, total, upper)
            for s in range(source_rows):
                gathered[block, s] = total[s]
            return carried

        lax.fori_loop(0, col_count, one_block, 0)
        return carried

    lax.fori_loop(0, row_count // row_pair, from_columns, 0)

    for col_step in reversed(range(col_count)):
        block = partner(my_col, col_step, col_count)
        sums_out[1, block] = fold([gathered[block, s] for s in range(source_rows)], jnp.add, sub)
        if col_step:
            start(
                sums_out.at[1, block],
                sums_in.at[my_col],
                col_send.at[col_step],
                col_recv.at[my_col],
                {"row": my_row, "col": block},
            )
    summed = sums_out[1, my_col]
    for col_step in range(1, col_count):
        other = partner(my_col, col_step, col_count)
        arrived(sums_in.at[other], col_recv.at[other], {"row": my_row, "col": other})
        summed += sums_in[other]
    own_source = source_mask((my_row * col_count + my_col) * tile_side)
    packed[2] = jnp.where(own_source, 0.0, lower[1, my_row] * summed)
    for copy in pending:
        copy.wait_send()


def unpack(packed, dist_out, path_out, cent_out):
    dist_out[...] = packed[0]
    path_out[...] = packed[1]
    cent_out[...] = jnp.sum(packed[2], axis=0, keepdims=True) / packed.shape[1]


def solution(mesh):
    row_count = mesh.shape["row"]
    col_count = mesh.shape["col"]

    def per_device(tiles, tile_index, tile_count, sources):
        slot_total, tile_side = tiles.shape[0], tiles.shape[1]
        source_rows = sources.shape[0]
        wide = (source_rows, tile_side)
        positions = row_count * col_count
        longest = max(row_count, col_count)
        mask_shape = (positions, tile_side // SUB, source_rows, SUB, tile_side)
        if positions > MASK_TILES:
            mask_shape = (1, 1, 1, SUB, tile_side)
        vector = pl.BlockSpec(memory_space=pltpu.VMEM)
        packed = pl.pallas_call(
            functools.partial(body, row_count, col_count),
            out_shape=jax.ShapeDtypeStruct((3,) + wide, jnp.float32),
            in_specs=[pl.BlockSpec(memory_space=pl.ANY)] * 4,
            out_specs=vector,
            scratch_shapes=[
                pltpu.SMEM((2, slot_total), jnp.int32),
                pltpu.SMEM((1,), jnp.int32),
                pltpu.SMEM((source_rows,), jnp.int32),
                pltpu.VMEM((slot_total, tile_side, tile_side), jnp.float32),
                pltpu.SMEM((positions,), jnp.int32),
                pltpu.VMEM((positions, tile_side, tile_side), jnp.float32),
                pltpu.VMEM((positions, tile_side, tile_side), jnp.float32),
                pltpu.VMEM((4 * source_rows, source_rows * tile_side), jnp.bfloat16),
                pltpu.VMEM((longest, tile_side, source_rows * tile_side), jnp.float32),
                pltpu.VMEM((longest, tile_side, source_rows * tile_side), jnp.float32),
                pltpu.VMEM(mask_shape, jnp.float32),
                pltpu.VMEM((longest, source_rows, SUB, tile_side), jnp.float32),
                pltpu.VMEM((LEVELS, row_count) + wide, jnp.float32),
                pltpu.VMEM((LEVELS - 1, row_count) + wide, jnp.float32),
                pltpu.VMEM((LEVELS, col_count, row_count) + wide, jnp.float32),
                pltpu.VMEM((col_count, row_count) + wide, jnp.float32),
                pltpu.VMEM((row_count, row_count) + wide, jnp.float32),
                pltpu.VMEM((row_count, row_count) + wide, jnp.float32),
                pltpu.VMEM((col_count,) + wide, jnp.float32),
                pltpu.VMEM((2, row_count) + wide, jnp.float32),
                pltpu.VMEM((BACK, col_count) + wide, jnp.float32),
                pltpu.VMEM((row_count, col_count) + wide, jnp.float32),
                pltpu.VMEM((col_count,) + wide, jnp.float32),
                pltpu.SemaphoreType.DMA,
                pltpu.SemaphoreType.DMA((3,)),
                pltpu.SemaphoreType.DMA((LEVELS + 2, row_count, col_count)),
                pltpu.SemaphoreType.DMA((LEVELS + 2, row_count, col_count)),
                pltpu.SemaphoreType.DMA((2, row_count)),
                pltpu.SemaphoreType.DMA((2, row_count)),
                pltpu.SemaphoreType.DMA((col_count,)),
                pltpu.SemaphoreType.DMA((col_count,)),
            ],
            compiler_params=pltpu.CompilerParams(
                collective_id=0,
                has_side_effects=True,
            ),
        )(tile_index.T, tile_count, sources, tiles)
        distance, paths, centrality = pl.pallas_call(
            unpack,
            out_shape=(
                jax.ShapeDtypeStruct(wide, jnp.float32),
                jax.ShapeDtypeStruct(wide, jnp.float32),
                jax.ShapeDtypeStruct((1, tile_side), jnp.float32),
            ),
            in_specs=[vector],
            out_specs=(vector, vector, vector),
        )(packed)
        return distance, paths, centrality.reshape(tile_side)

    in_specs = (
        P(("groups", "row", "col"), None, None),
        P(("groups", "row", "col"), None),
        P(("groups", "row", "col")),
        P("groups"),
    )
    out_specs = (
        P("groups", ("row", "col")),
        P("groups", ("row", "col")),
        P(("groups", "row", "col")),
    )
    return jax.shard_map(
        per_device, mesh=mesh, in_specs=in_specs, out_specs=out_specs, check_vma=False
    )
```

time: 38.5 us -> 34.7 us (0.901)
  Pallas kernels: 36.9 us -> 33.1 us
    pallas_call x1, Pallas kernels: 35.6 us -> 31.8 us  [per_device(): pl.pallas_call(functools.partial(body, row_count, col_count), out_shape=j...]
where the time goes in v1:
time: 34.7 us; the launch traced here: 34.4 us
  Pallas kernels  33.1 us (95%)
  between operations  1.29 us (4%)
    pallas_call x1, Pallas kernels, per_device(): pl.pallas_call(functools.partial(body, row_count, col_count), out_shape=j...  31.8 us
    pallas_call x1, Pallas kernels, per_device(): pl.pallas_call(unpack, out_shape=(jax.ShapeDtypeStruct(wide, jnp.float32)...  1.31 us

profile of v1, /device:TPU:0, one launch (start us, length us, event | category | flops | bytes accessed | tf_op | source)
XLA Modules:
  0.0 34.4 jit_solution(6789466773749566181)
XLA Ops:
  1.3 31.8 %shard_map.67.packed = f32[3,8,128]{2,1,0:T(8,128)} custom-call(s32[2,16]{1,0:T(2,128)} %bitcast.2, s32[1]{0:T(128)S(6)} %copy.7.count_hbm, s32[8]{0:T(128)} %source_hbm.1, f32[16,128,128]{2,1,0:T(8,128)} %tiles_ref.1), custom_call_target="tpu_custom_call" | custom-call | tf_op jit(solution)/shard_map/pallas_call | solution.py:636
  33.1 1.3 %shard_map.68 = (f32[8,128]{1,0:T(8,128)}, f32[8,128]{1,0:T(8,128)}, f32[1,128]{1,0:T(1,128)}) custom-call(f32[3,8,128]{2,1,0:T(8,128)} %shard_map.67.packed), custom_call_target="tpu_custom_call" | custom-call | tf_op jit(solution)/shard_map/pallas_call | solution.py:679

commit v2 on v1

--- a/solution.py
+++ b/solution.py
@@ -57,12 +57,10 @@
     row_count,
     col_count,
     index_hbm,
-    count_hbm,
     source_hbm,
     tiles_ref,
     packed,
     index_ref,
-    count_ref,
     source_ref,
     raw,
     place_ref,
@@ -70,8 +68,11 @@
     weights_back,
     pick,
     lanes,
-    lanes_more,
+    lanes_even,
+    lanes_odd,
+    rows,
     masks,
+    weighted,
     gathered,
     dist_out,
     count_out,
@@ -99,12 +100,12 @@
     my_col = lax.axis_index("col")
     positions = row_count * col_count
     row_chunk = CHUNK if row_count % CHUNK == 0 else 1
+    col_chunk = CHUNK if col_count % CHUNK == 0 else 1
     row_pair = PAIR if row_count % PAIR == 0 else 1
-    col_pair = PAIR if col_count % PAIR == 0 else 1
     groups = tile_side // SUB
     wide = (source_rows, tile_side)
     last = LEVELS - 1
-    keep_masks = masks.shape[0] == positions
+    keep_masks = masks.shape[0] > 1
     pending = []
 
     def others():
@@ -120,8 +121,7 @@
 
     small = [
         pltpu.make_async_copy(index_hbm, index_ref, small_sem.at[0]),
-        pltpu.make_async_copy(count_hbm, count_ref, small_sem.at[1]),
-        pltpu.make_async_copy(source_hbm, source_ref, small_sem.at[2]),
+        pltpu.make_async_copy(source_hbm, source_ref, small_sem.at[1]),
     ]
     for copy in small:
         copy.start()
@@ -223,31 +223,65 @@
         )
         return best, total
 
+    def cut(value):
+        high = value.astype(jnp.bfloat16).astype(jnp.float32)
+        rest = value - high
+        middle = rest.astype(jnp.bfloat16).astype(jnp.float32)
+        return jnp.concatenate([high, middle, rest - middle, jnp.zeros_like(high)], axis=0)
+
     def spread(value, target):
-        scaled = value * scale_up
-        high = scaled.astype(jnp.bfloat16).astype(jnp.float32)
-        rest = scaled - high
-        middle = rest.astype(jnp.bfloat16).astype(jnp.float32)
-        pieces = jnp.concatenate([high, middle, rest - middle, jnp.zeros_like(high)], axis=0)
         target[...] = lax.dot_general(
-            pieces.astype(jnp.bfloat16),
+            cut(value * scale_up).astype(jnp.bfloat16),
             pick[...],
             (((0,), (0,)), ((), ())),
             preferred_element_type=jnp.float32,
         )
 
-    def spread_at(ref, place, group, s):
-        return ref[
-            place, group * SUB : (group + 1) * SUB, s * tile_side : (s + 1) * tile_side
-        ]
+    def deal(value, target):
+        pieces = cut(value)
+        owner = lax.broadcasted_iota(jnp.int32, pieces.shape, 0) % source_rows
+        for s in range(source_rows):
+            target[:, s * tile_side : (s + 1) * tile_side] = jnp.where(
+                owner == s, pieces, 0.0
+            ).astype(jnp.bfloat16)
+
+    def join(block):
+        parts = [weighted[block, k * source_rows : (k + 1) * source_rows, :] for k in range(3)]
+        return parts[0] + (parts[1] + parts[2])
+
+    def add_weighted(columns, block):
+        total = weighted[block]
+        for column in columns:
+            if keep_masks:
+                total += jnp.dot(
+                    rows[column], masks[block, column], preferred_element_type=jnp.float32
+                )
+            else:
+                for s in range(source_rows):
+                    total += jnp.dot(
+                        rows[column, :, s * tile_side : (s + 1) * tile_side],
+                        same_behind(block, column, s),
+                        preferred_element_type=jnp.float32,
+                    )
+        weighted[block] = total
+
+    def repeat(count, one):
+        if count == 1:
+            one(0)
+        else:
+
+            def step(place, carried):
+                one(place)
+                return carried
+
+            lax.fori_loop(0, count, step, 0)
+
+    def spread_at(ref, group, s):
+        return ref[group * SUB : (group + 1) * SUB, s * tile_side : (s + 1) * tile_side]
 
     for copy in small:
         copy.wait()
-    live_count = count_ref[0]
-    holds = []
-    for slot in range(slot_total):
-        position = index_ref[0, slot] * row_count + index_ref[1, slot]
-        holds.append(jnp.where(slot < live_count, position, -1))
+    holds = [index_ref[0, slot] * row_count + index_ref[1, slot] for slot in range(slot_total)]
 
     def find_slot(position, carried):
         found = jnp.int32(-1)
@@ -303,7 +337,7 @@
     lax.fori_loop(0, positions, turn, 0)
 
     def relax(block):
-        def columns(chunk, carried):
+        def columns(chunk):
             first = chunk * row_chunk
             best = [[gathered[first + t, s] for s in range(source_rows)] for t in range(row_chunk)]
             for group in range(groups):
@@ -312,43 +346,50 @@
                     for t in range(row_chunk)
                 ]
                 for s in range(source_rows):
-                    near = spread_at(lanes, block, group, s)
+                    near = spread_at(lanes.at[block], group, s)
                     for t in range(row_chunk):
                         best[t][s] = jnp.minimum(best[t][s], near + lines[t])
             for t in range(row_chunk):
                 for s in range(source_rows):
                     gathered[first + t, s] = best[t][s]
-            return carried
-
-        lax.fori_loop(0, row_count // row_chunk, columns, 0)
-
-    def tally(level, block):
-        def columns(chunk, carried):
-            first = chunk * row_pair
-            total = [[gathered[first + t, s] for s in range(source_rows)] for t in range(row_pair)]
-            best = [
-                [
-                    jnp.broadcast_to(dist_out[level, first + t, s : s + 1, :], (SUB, tile_side))
-                    for s in range(source_rows)
-                ]
+
+        repeat(row_count // row_chunk, columns)
+
+    def tally(level, block, shares):
+        def columns(chunk):
+            for first in range(0, row_chunk, row_pair):
+                tally_pair(level, block, shares, chunk * row_chunk + first)
+
+        repeat(row_count // row_chunk, columns)
+
+    def tally_pair(level, block, shares, first):
+        total = [[gathered[first + t, s] for s in range(source_rows)] for t in range(row_pair)]
+        best = [
+            [
+                jnp.broadcast_to(dist_out[level, first + t, s : s + 1, :], (SUB, tile_side))
+                for s in range(source_rows)
+            ]
+            for t in range(row_pair)
+        ]
+        for group in range(groups):
+            lines = [
+                weights[block * row_count + first + t, group * SUB : (group + 1) * SUB, :]
                 for t in range(row_pair)
             ]
-            for group in range(groups):
-                lines = [
-                    weights[block * row_count + first + t, group * SUB : (group + 1) * SUB, :]
-                    for t in range(row_pair)
-                ]
-                for s in range(source_rows):
-                    near = spread_at(lanes, block, group, s)
-                    paths = 1.0 if level == 1 else spread_at(lanes_more, block, group, s)
-                    for t in range(row_pair):
-                        total[t][s] += jnp.where(near + lines[t] == best[t][s], paths, 0.0)
-            for t in range(row_pair):
-                for s in range(source_rows):
-                    gathered[first + t, s] = total[t][s]
-            return carried
-
-        lax.fori_loop(0, row_count // row_pair, columns, 0)
+            for s in range(source_rows):
+                near = spread_at(lanes.at[block], group, s)
+                paths = 1.0 if shares is None else spread_at(shares, group, s)
+                for t in range(row_pair):
+                    total[t][s] += jnp.where(near + lines[t] == best[t][s], paths, 0.0)
+        for t in range(row_pair):
+            for s in range(source_rows):
+                gathered[first + t, s] = total[t][s]
+
+    def same_behind(block, column, s):
+        below = lanes[column, :, s * tile_side : (s + 1) * tile_side]
+        upper = band[block, s : s + 1, :]
+        same = upper + weights_back[block * row_count + column] == below
+        return jnp.where(same, 1.0, 0.0).astype(jnp.bfloat16)
 
     def fill(count, value):
         def one(place, carried):
@@ -358,19 +399,42 @@
 
         lax.fori_loop(0, count, one, 0)
 
+    def block_source(block):
+        return source_mask((my_row * col_count + block) * tile_side)
+
+    def spread_dist(level, block):
+        best = nearest([dist_in[level - 1, block, g] for g in range(row_count)])
+        spread(jnp.where(block_source(block), 0.0, best), lanes.at[block])
+
+    def wait_count(block, own):
+        block_arrived(LEVELS, count_in, block, own)
+
+    def spread_count(level, block, target):
+        found = combine(
+            [dist_in[level - 1, block, g] for g in range(row_count)],
+            [count_in[block, g] for g in range(row_count)],
+        )
+        spread(settle(*found, block_source(block))[1], target)
+
     def forward(level):
         fill(row_count, far_value)
+        final = partner(my_col, col_count - 1, col_count)
 
         def relax_block(step, carried):
             block = partner(my_col, step, col_count)
             block_arrived(level - 1, dist_in.at[level - 1], block, step == 0)
-            best = nearest([dist_in[level - 1, block, g] for g in range(row_count)])
-            is_source = source_mask((my_row * col_count + block) * tile_side)
-            spread(jnp.where(is_source, 0.0, best), lanes.at[block])
+            spread_dist(level, block)
             relax(block)
             return carried
 
-        lax.fori_loop(0, col_count, relax_block, 0)
+        lax.fori_loop(0, col_count - 1, relax_block, 0)
+        block_arrived(level - 1, dist_in.at[level - 1], final, None if col_count > 1 else True)
+        if level > 1:
+            wait_count(my_col, True)
+        spread_dist(level, final)
+        if level > 1:
+            spread_count(level, my_col, lanes_even)
+        relax(final)
 
         def close_dist(column, carried):
             dist_out[level, column] = fold(
@@ -391,24 +455,32 @@
         )
 
         fill(row_count, 0.0)
-
-        def tally_blocks(pair, carried):
-            blocks = [partner(my_col, pair * col_pair + t, col_count) for t in range(col_pair)]
-            if level > 1:
-                for t, block in enumerate(blocks):
-                    block_arrived(LEVELS, count_in, block, (pair == 0) if t == 0 else None)
-                for block in blocks:
-                    found = combine(
-                        [dist_in[level - 1, block, g] for g in range(row_count)],
-                        [count_in[block, g] for g in range(row_count)],
-                    )
-                    is_source = source_mask((my_row * col_count + block) * tile_side)
-                    spread(settle(*found, is_source)[1], lanes_more.at[block])
-            for block in blocks:
-                tally(level, block)
-            return carried
-
-        lax.fori_loop(0, col_count // col_pair, tally_blocks, 0)
+        if level > 1:
+
+            def tally_next(step, shares, following_shares):
+                following = partner(my_col, step + 1, col_count)
+                wait_count(following, None)
+                spread_count(level, following, following_shares)
+                tally(level, partner(my_col, step, col_count), shares)
+
+            def tally_two(pair):
+                tally_next(2 * pair, lanes_even, lanes_odd)
+                tally_next(2 * pair + 1, lanes_odd, lanes_even)
+
+            if col_count > 2:
+                repeat((col_count - 1) // 2, tally_two)
+            if col_count % 2:
+                tally(level, final, lanes_even)
+            else:
+                tally_next(col_count - 2, lanes_even, lanes_odd)
+                tally(level, final, lanes_odd)
+        else:
+
+            def tally_block(block, carried):
+                tally(level, block, None)
+                return carried
+
+            lax.fori_loop(0, col_count, tally_block, 0)
 
         def close_count(column, carried):
             total = fold([gathered[column, s] for s in range(source_rows)], jnp.add, sub)
@@ -457,16 +529,6 @@
         is_source = source_mask((my_row * col_count + block) * tile_side)
         band[block] = jnp.where(is_source, 0.0, best)
 
-    def upper_lines(block):
-        return [
-            jnp.broadcast_to(band[block, s : s + 1, :], (SUB, tile_side)) for s in range(source_rows)
-        ]
-
-    def compare(block, column, group, upper, visit):
-        line = weights_back[block * row_count + column, group * SUB : (group + 1) * SUB, :]
-        for s in range(source_rows):
-            visit(s, upper[s] + line == spread_at(lanes, column, group, s))
-
     for col_step in range(col_count):
         block = partner(my_col, col_step, col_count)
         if col_step:
@@ -475,37 +537,20 @@
             band[block] = lower[0, my_row]
         if keep_masks:
 
-            def mark(column, carried, block=block):
-                upper = upper_lines(block)
-                for group in range(groups):
-
-                    def keep(s, same, group=group):
-                        masks[block * row_count + column, group, s] = jnp.where(same, 1.0, 0.0)
-
-                    compare(block, column, group, upper, keep)
+            def keep(column, carried, block=block):
+                for s in range(source_rows):
+                    masks[block, column, s * tile_side : (s + 1) * tile_side, :] = same_behind(
+                        block, column, s
+                    )
                 return carried
 
-            lax.fori_loop(0, row_count, mark, 0)
-
-    def add_shares(block, column, total, upper):
-        for group in range(groups):
-            if keep_masks:
-                for s in range(source_rows):
-                    share = spread_at(lanes_more, column, group, s)
-                    total[s] += masks[block * row_count + column, group, s] * share
-            else:
-
-                def add(s, same, group=group):
-                    share = spread_at(lanes_more, column, group, s)
-                    total[s] += jnp.where(same, share, 0.0)
-
-                compare(block, column, group, upper, add)
+            lax.fori_loop(0, row_count, keep, 0)
 
     def coefficient(column, dependency):
         paths = lower[1, column]
-        spread(
+        deal(
             jnp.where(paths > 0.5, (1.0 + dependency) / jnp.maximum(paths, 1.0), 0.0),
-            lanes_more.at[column],
+            rows.at[column],
         )
 
     full_arrived(1, full_count)
@@ -524,21 +569,15 @@
 
     lax.fori_loop(0, row_count // row_chunk, lower_paths, 0)
 
+    weighted[...] = jnp.zeros_like(weighted)
     for col_step in reversed(range(col_count)):
         block = partner(my_col, col_step, col_count)
 
-        def first_sums(column, total, block=block):
-            total = list(total)
-            add_shares(block, column, total, None if keep_masks else upper_lines(block))
-            return tuple(total)
-
-        total = lax.fori_loop(
-            0,
-            row_count,
-            first_sums,
-            tuple(jnp.zeros((SUB, tile_side), jnp.float32) for _ in range(source_rows)),
-        )
-        sums_out[0, block] = fold(list(total), jnp.add, sub)
+        def first_sums(chunk, block=block):
+            add_weighted([chunk * row_chunk + t for t in range(row_chunk)], block)
+
+        repeat(row_count // row_chunk, first_sums)
+        sums_out[0, block] = join(block)
         for row_step in reversed(range(row_count)):
             if row_step or col_step:
                 other = partner(my_row, row_step, row_count)
@@ -554,7 +593,7 @@
 
     packed[0] = jnp.where(lower[0, my_row] < half_far, lower[0, my_row], -1.0)
     packed[1] = lower[1, my_row]
-    fill(col_count, 0.0)
+    weighted[...] = jnp.zeros_like(weighted)
 
     def from_columns(pair, carried):
         columns = [partner(my_row, pair * row_pair + t, row_count) for t in range(row_pair)]
@@ -577,23 +616,19 @@
             summed = functools.reduce(jnp.add, [sums_all[column, g] for g in range(col_count)])
             coefficient(column, lower[1, column] * summed)
 
-        def one_block(block, carried):
-            total = [gathered[block, s] for s in range(source_rows)]
-            upper = None if keep_masks else upper_lines(block)
-            for column in columns:
-                add_shares(block, column, total, upper)
-            for s in range(source_rows):
-                gathered[block, s] = total[s]
-            return carried
-
-        lax.fori_loop(0, col_count, one_block, 0)
+        def some_blocks(chunk):
+            for t in range(col_chunk):
+                add_weighted(columns, chunk * col_chunk + t)
+
+        repeat(col_count // col_chunk, some_blocks)
         return carried
 
     lax.fori_loop(0, row_count // row_pair, from_columns, 0)
 
+    early = len(pending)
     for col_step in reversed(range(col_count)):
         block = partner(my_col, col_step, col_count)
-        sums_out[1, block] = fold([gathered[block, s] for s in range(source_rows)], jnp.add, sub)
+        sums_out[1, block] = join(block)
         if col_step:
             start(
                 sums_out.at[1, block],
@@ -602,6 +637,8 @@
                 col_recv.at[my_col],
                 {"row": my_row, "col": block},
             )
+    for copy in pending[:early]:
+        copy.wait_send()
     summed = sums_out[1, my_col]
     for col_step in range(1, col_count):
         other = partner(my_col, col_step, col_count)
@@ -609,7 +646,7 @@
         summed += sums_in[other]
     own_source = source_mask((my_row * col_count + my_col) * tile_side)
     packed[2] = jnp.where(own_source, 0.0, lower[1, my_row] * summed)
-    for copy in pending:
+    for copy in pending[early:]:
         copy.wait_send()
 
 
@@ -624,23 +661,23 @@
     col_count = mesh.shape["col"]
 
     def per_device(tiles, tile_index, tile_count, sources):
+        del tile_count
         slot_total, tile_side = tiles.shape[0], tiles.shape[1]
         source_rows = sources.shape[0]
         wide = (source_rows, tile_side)
         positions = row_count * col_count
         longest = max(row_count, col_count)
-        mask_shape = (positions, tile_side // SUB, source_rows, SUB, tile_side)
+        mask_shape = (col_count, row_count, source_rows * tile_side, tile_side)
         if positions > MASK_TILES:
-            mask_shape = (1, 1, 1, SUB, tile_side)
+            mask_shape = (1, 1, 2 * SUB, tile_side)
         vector = pl.BlockSpec(memory_space=pltpu.VMEM)
         packed = pl.pallas_call(
             functools.partial(body, row_count, col_count),
-            out_shape=jax.ShapeDtypeStruct((3,) + wide, jnp.float32),
-            in_specs=[pl.BlockSpec(memory_space=pl.ANY)] * 4,
+            out_shape=pltpu.VMEM((3,) + wide, jnp.float32),
+            in_specs=[pl.BlockSpec(memory_space=pl.ANY)] * 3,
             out_specs=vector,
             scratch_shapes=[
                 pltpu.SMEM((2, slot_total), jnp.int32),
-                pltpu.SMEM((1,), jnp.int32),
                 pltpu.SMEM((source_rows,), jnp.int32),
                 pltpu.VMEM((slot_total, tile_side, tile_side), jnp.float32),
                 pltpu.SMEM((positions,), jnp.int32),
@@ -648,8 +685,11 @@
                 pltpu.VMEM((positions, tile_side, tile_side), jnp.float32),
                 pltpu.VMEM((4 * source_rows, source_rows * tile_side), jnp.bfloat16),
                 pltpu.VMEM((longest, tile_side, source_rows * tile_side), jnp.float32),
-                pltpu.VMEM((longest, tile_side, source_rows * tile_side), jnp.float32),
-                pltpu.VMEM(mask_shape, jnp.float32),
+                pltpu.VMEM((tile_side, source_rows * tile_side), jnp.float32),
+                pltpu.VMEM((tile_side, source_rows * tile_side), jnp.float32),
+                pltpu.VMEM((longest, 4 * source_rows, source_rows * tile_side), jnp.bfloat16),
+                pltpu.VMEM(mask_shape, jnp.bfloat16),
+                pltpu.VMEM((col_count, 4 * source_rows, tile_side), jnp.float32),
                 pltpu.VMEM((longest, source_rows, SUB, tile_side), jnp.float32),
                 pltpu.VMEM((LEVELS, row_count) + wide, jnp.float32),
                 pltpu.VMEM((LEVELS - 1, row_count) + wide, jnp.float32),
@@ -663,7 +703,7 @@
                 pltpu.VMEM((row_count, col_count) + wide, jnp.float32),
                 pltpu.VMEM((col_count,) + wide, jnp.float32),
                 pltpu.SemaphoreType.DMA,
-                pltpu.SemaphoreType.DMA((3,)),
+                pltpu.SemaphoreType.DMA((2,)),
                 pltpu.SemaphoreType.DMA((LEVELS + 2, row_count, col_count)),
                 pltpu.SemaphoreType.DMA((LEVELS + 2, row_count, col_count)),
                 pltpu.SemaphoreType.DMA((2, row_count)),
@@ -675,7 +715,7 @@
                 collective_id=0,
                 has_side_effects=True,
             ),
-        )(tile_index.T, tile_count, sources, tiles)
+        )(tile_index.T, sources, tiles)
         distance, paths, centrality = pl.pallas_call(
             unpack,
             out_shape=(
@@ -685,6 +725,7 @@
             ),
             in_specs=[vector],
             out_specs=(vector, vector, vector),
+            compiler_params=pltpu.CompilerParams(vmem_limit_bytes=2**20),
         )(packed)
         return distance, paths, centrality.reshape(tile_side)
 

time: 34.7 us -> 31.6 us (0.911)
  Pallas kernels: 33.1 us -> 30.8 us
  between operations: 1.29 us -> 0.64 us
    pallas_call x1, Pallas kernels: 31.8 us -> 30.2 us  [per_device(): pl.pallas_call(functools.partial(body, row_count, col_count), out_shape=p...]
    pallas_call x1, Pallas kernels: 1.31 us -> 0.6 us  [per_device(): pl.pallas_call(unpack, out_shape=(jax.ShapeDtypeStruct(wide, jnp.float32)...]
where the time goes in v2:
time: 31.6 us; the launch traced here: 31.4 us
  Pallas kernels  30.8 us (97%)
  between operations  0.64 us (2%)
    pallas_call x1, Pallas kernels, per_device(): pl.pallas_call(functools.partial(body, row_count, col_count), out_shape=p...  30.2 us

profile of v2, /device:TPU:0, one launch (start us, length us, event | category | flops | bytes accessed | tf_op | source)
XLA Modules:
  0.0 31.4 jit_solution(17289715304866959168)
XLA Ops:
  0.6 30.2 %shard_map.58.packed = f32[3,8,128]{2,1,0:T(8,128)S(1)} custom-call(s32[2,16]{1,0:T(2,128)} %bitcast.2, s32[8]{0:T(128)} %source_hbm.1, f32[16,128,128]{2,1,0:T(8,128)} %tiles_ref.1), custom_call_target="tpu_custom_call" | custom-call | tf_op jit(solution)/shard_map/pallas_call | solution.py:674
  30.8 0.6 %shard_map.59 = (f32[8,128]{1,0:T(8,128)}, f32[8,128]{1,0:T(8,128)}, f32[1,128]{1,0:T(1,128)}) custom-call(f32[3,8,128]{2,1,0:T(8,128)S(1)} %shard_map.58.packed), custom_call_target="tpu_custom_call" | custom-call | tf_op jit(solution)/shard_map/pallas_call | solution.py:719

commit v3 on v2

--- a/solution.py
+++ b/solution.py
@@ -148,16 +148,15 @@
         copy.start()
         pending.append(copy)
 
-    def push_all(stage, source_of, target, with_own_col=True):
+    def push_all(stage, source_of, target):
         for other_row, other_col, row_step, col_step in others():
-            if col_step or with_own_col:
-                start(
-                    source_of(other_row, other_col),
-                    target,
-                    all_send.at[stage, row_step, col_step],
-                    all_recv.at[stage, my_row, my_col],
-                    {"row": other_row, "col": other_col},
-                )
+            start(
+                source_of(other_row, other_col),
+                target,
+                all_send.at[stage, row_step, col_step],
+                all_recv.at[stage, my_row, my_col],
+                {"row": other_row, "col": other_col},
+            )
 
     def push_full(stage, source, target):
         target[my_row] = source[...]
@@ -337,23 +336,32 @@
     lax.fori_loop(0, positions, turn, 0)
 
     def relax(block):
+        near = lanes.at[block]
+
         def columns(chunk):
             first = chunk * row_chunk
-            best = [[gathered[first + t, s] for s in range(source_rows)] for t in range(row_chunk)]
-            for group in range(groups):
-                lines = [
-                    weights[block * row_count + first + t, group * SUB : (group + 1) * SUB, :]
-                    for t in range(row_chunk)
-                ]
-                for s in range(source_rows):
-                    near = spread_at(lanes.at[block], group, s)
+            for s in range(source_rows):
+                best = [gathered[first + t, s] for t in range(row_chunk)]
+                for group in range(groups):
+                    value = spread_at(near, group, s)
                     for t in range(row_chunk):
-                        best[t][s] = jnp.minimum(best[t][s], near + lines[t])
-            for t in range(row_chunk):
-                for s in range(source_rows):
-                    gathered[first + t, s] = best[t][s]
+                        line = weights[
+                            block * row_count + first + t, group * SUB : (group + 1) * SUB, :
+                        ]
+                        best[t] = jnp.minimum(best[t], value + line)
+                for t in range(row_chunk):
+                    gathered[first + t, s] = best[t]
 
         repeat(row_count // row_chunk, columns)
+
+    def relax_column(level, block, column):
+        near = lanes.at[block]
+        best = [gathered[column, s] for s in range(source_rows)]
+        for group in range(groups):
+            line = weights[block * row_count + column, group * SUB : (group + 1) * SUB, :]
+            for s in range(source_rows):
+                best[s] = jnp.minimum(best[s], spread_at(near, group, s) + line)
+        dist_out[level, column] = fold(best, jnp.minimum, sub)
 
     def tally(level, block, shares):
         def columns(chunk):
@@ -434,25 +442,22 @@
         spread_dist(level, final)
         if level > 1:
             spread_count(level, my_col, lanes_even)
-        relax(final)
-
-        def close_dist(column, carried):
-            dist_out[level, column] = fold(
-                [gathered[column, s] for s in range(source_rows)], jnp.minimum, sub
-            )
-            return carried
-
-        lax.fori_loop(0, row_count, close_dist, 0)
+        for row_step in reversed(range(row_count)):
+            column = partner(my_row, row_step, row_count)
+            relax_column(level, final, column)
+            for col_step in reversed(range(col_count)):
+                if (row_step or col_step) and (col_step or level != last):
+                    start(
+                        dist_out.at[level, column],
+                        dist_in.at[level, my_col, my_row],
+                        all_send.at[level, row_step, col_step],
+                        all_recv.at[level, my_row, my_col],
+                        {"row": column, "col": partner(my_col, col_step, col_count)},
+                    )
         if level == last:
             push_full(0, dist_out.at[level], full_dist)
         else:
             dist_in[level, my_col, my_row] = dist_out[level, my_row]
-        push_all(
-            level,
-            lambda other_row, other_col: dist_out.at[level, other_row],
-            dist_in.at[level, my_col, my_row],
-            level != last,
-        )
 
         fill(row_count, 0.0)
         if level > 1:
@@ -460,8 +465,8 @@
             def tally_next(step, shares, following_shares):
                 following = partner(my_col, step + 1, col_count)
                 wait_count(following, None)
+                tally(level, partner(my_col, step, col_count), shares)
                 spread_count(level, following, following_shares)
-                tally(level, partner(my_col, step, col_count), shares)
 
             def tally_two(pair):
                 tally_next(2 * pair, lanes_even, lanes_odd)
@@ -595,7 +600,7 @@
     packed[1] = lower[1, my_row]
     weighted[...] = jnp.zeros_like(weighted)
 
-    def from_columns(pair, carried):
+    def settle_columns(pair, own):
         columns = [partner(my_row, pair * row_pair + t, row_count) for t in range(row_pair)]
         for t, column in enumerate(columns):
             for col_step in range(col_count):
@@ -608,13 +613,17 @@
                         {"row": column, "col": giver},
                     )
 
-                if col_step == 0 and t == 0:
-                    pl.when(pair > 0)(wait)
+                if col_step == 0 and t == 0 and own is not None:
+                    pl.when(jnp.logical_not(own))(wait)
                 else:
                     wait()
         for column in columns:
             summed = functools.reduce(jnp.add, [sums_all[column, g] for g in range(col_count)])
             coefficient(column, lower[1, column] * summed)
+        return columns
+
+    def from_columns(pair, carried):
+        columns = settle_columns(pair, pair == 0)
 
         def some_blocks(chunk):
             for t in range(col_chunk):
@@ -623,11 +632,13 @@
         repeat(col_count // col_chunk, some_blocks)
         return carried
 
-    lax.fori_loop(0, row_count // row_pair, from_columns, 0)
-
+    pairs = row_count // row_pair
+    lax.fori_loop(0, pairs - 1, from_columns, 0)
+    columns = settle_columns(pairs - 1, None if pairs > 1 else True)
     early = len(pending)
     for col_step in reversed(range(col_count)):
         block = partner(my_col, col_step, col_count)
+        add_weighted(columns, block)
         sums_out[1, block] = join(block)
         if col_step:
             start(

time: 31.6 us -> 31.1 us (0.984)
  Pallas kernels: 30.8 us -> 30.3 us
    pallas_call x1, Pallas kernels: 30.2 us -> 29.7 us  [per_device(): pl.pallas_call(functools.partial(body, row_count, col_count), out_shape=p...]
where the time goes in v3:
time: 31.1 us; the launch traced here: 30.9 us
  Pallas kernels  30.3 us (97%)
  between operations  0.64 us (2%)
    pallas_call x1, Pallas kernels, per_device(): pl.pallas_call(functools.partial(body, row_count, col_count), out_shape=p...  29.7 us

profile of v3, /device:TPU:0, one launch (start us, length us, event | category | flops | bytes accessed | tf_op | source)
XLA Modules:
  0.0 30.9 jit_solution(17637886849004639551)
XLA Ops:
  0.6 29.7 %shard_map.58.packed = f32[3,8,128]{2,1,0:T(8,128)S(1)} custom-call(s32[2,16]{1,0:T(2,128)} %bitcast.2, s32[8]{0:T(128)} %source_hbm.1, f32[16,128,128]{2,1,0:T(8,128)} %tiles_ref.1), custom_call_target="tpu_custom_call" | custom-call | tf_op jit(solution)/shard_map/pallas_call | solution.py:685
  30.3 0.6 %shard_map.59 = (f32[8,128]{1,0:T(8,128)}, f32[8,128]{1,0:T(8,128)}, f32[1,128]{1,0:T(1,128)}) custom-call(f32[3,8,128]{2,1,0:T(8,128)S(1)} %shard_map.58.packed), custom_call_target="tpu_custom_call" | custom-call | tf_op jit(solution)/shard_map/pallas_call | solution.py:730

commit v4 on v3

--- a/solution.py
+++ b/solution.py
@@ -510,7 +510,10 @@
 
     full_arrived(0, full_dist)
 
-    def lower_dist(chunk, carried):
+    own_best = nearest([full_dist[g, my_row] for g in range(row_count)])
+    band[my_col] = jnp.where(block_source(my_col), 0.0, own_best)
+
+    def lower_dist(chunk):
         for t in range(row_chunk):
             column = chunk * row_chunk + t
             best = nearest([full_dist[g, column] for g in range(row_count)])
@@ -518,9 +521,14 @@
             settled = jnp.where(is_source, 0.0, best)
             lower[0, column] = settled
             spread(settled, lanes.at[column])
-        return carried
-
-    lax.fori_loop(0, row_count // row_chunk, lower_dist, 0)
+        for t in range(row_chunk if keep_masks else 0):
+            column = chunk * row_chunk + t
+            for s in range(source_rows):
+                masks[my_col, column, s * tile_side : (s + 1) * tile_side, :] = same_behind(
+                    my_col, column, s
+                )
+
+    repeat(row_count // row_chunk, lower_dist)
 
     def settle_upper(block):
         for row_step in range(row_count):
@@ -534,12 +542,9 @@
         is_source = source_mask((my_row * col_count + block) * tile_side)
         band[block] = jnp.where(is_source, 0.0, best)
 
-    for col_step in range(col_count):
+    for col_step in range(1, col_count):
         block = partner(my_col, col_step, col_count)
-        if col_step:
-            settle_upper(block)
-        else:
-            band[block] = lower[0, my_row]
+        settle_upper(block)
         if keep_masks:
 
             def keep(column, carried, block=block):

time: 31.1 us -> 31.1 us (level)
  no operation moved by 1% of the time
where the time goes in v4:
time: 31.1 us; the launch traced here: 30.9 us
  Pallas kernels  30.3 us (97%)
  between operations  0.64 us (2%)
    pallas_call x1, Pallas kernels, per_device(): pl.pallas_call(functools.partial(body, row_count, col_count), out_shape=p...  29.7 us

profile of v4, /device:TPU:0, one launch (start us, length us, event | category | flops | bytes accessed | tf_op | source)
XLA Modules:
  0.0 30.9 jit_solution(12506371318387831572)
XLA Ops:
  0.6 29.7 %shard_map.58.packed = f32[3,8,128]{2,1,0:T(8,128)S(1)} custom-call(s32[2,16]{1,0:T(2,128)} %bitcast.2, s32[8]{0:T(128)} %source_hbm.1, f32[16,128,128]{2,1,0:T(8,128)} %tiles_ref.1), custom_call_target="tpu_custom_call" | custom-call | tf_op jit(solution)/shard_map/pallas_call | solution.py:690
  30.3 0.6 %shard_map.59 = (f32[8,128]{1,0:T(8,128)}, f32[8,128]{1,0:T(8,128)}, f32[1,128]{1,0:T(1,128)}) custom-call(f32[3,8,128]{2,1,0:T(8,128)S(1)} %shard_map.58.packed), custom_call_target="tpu_custom_call" | custom-call | tf_op jit(solution)/shard_map/pallas_call | solution.py:735
